TPU v7x, 32 devices: a whole 2x2x4 slice. The times are simulated.
32 devices in a mesh: dp: 8 (over y, x, core), tensor: 4 (over z).
Axes of the slice: x: 2, y: 2, z: 4, core: 2. Of those that a mesh axis runs over, the one named last changes fastest.
Arguments:
- tokens: bfloat16 [24, 256, 768], P('dp', 'tensor'), may hold values from -32 to 32
- counts: int32 [24, 4], P('dp'), may hold values from 1 to 64, 197 in all within a row
- w_qkv: bfloat16 [3, 768, 768], P(None, 'dp', 'tensor'), may hold values from -4 to 4
- b_qv: bfloat16 [2, 12, 64], P(None, 'tensor', 'dp'), may hold values from -3 to 3
- w_out: bfloat16 [768, 768], P('tensor', 'dp'), may hold values from -0.875 to 0.875
- w_fc1: bfloat16 [768, 3072], P('dp', 'tensor'), may hold values from -0.21875 to 0.21875
- b_fc1: bfloat16 [48, 64], P('tensor', 'dp'), may hold values from -3 to 3
- w_fc2: bfloat16 [3072, 768], P('tensor', 'dp'), may hold values from -0.109375 to 0.109375
- ln_gain: bfloat16 [2, 768], P(None, 'dp'), may hold values from 0.25 to 1.75
- vec_bias: bfloat16 [4, 768], P(None, 'dp'), may hold values from -3 to 3
- cotangent: bfloat16 [24, 256, 768], P('dp', 'tensor'), may hold values from -6 to 6
Outputs:
- out: bfloat16 [24, 256, 768], P('dp', 'tensor')
- grad_tokens: bfloat16 [24, 256, 768], P('dp', 'tensor')
- grad_qkv: float32 [3, 768, 768], P(None, 'dp', 'tensor')
- grad_out: float32 [768, 768], P('tensor', 'dp')
- grad_fc1: float32 [768, 3072], P('dp', 'tensor')
- grad_fc2: float32 [3072, 768], P('tensor', 'dp')
- grad_bqv: float32 [2, 12, 64], P(None, 'tensor', 'dp')
- grad_bfc1: float32 [48, 64], P('tensor', 'dp')
- grad_gain: float32 [2, 768], P(None, ('dp', 'tensor'))
- grad_vbias: float32 [4, 768], P(None, ('dp', 'tensor'))
Inputs may be any that keep to these rules, and one draw needn't show every extreme that they name: `counts`: row i lists how many of image i's 197 tokens each index of tensor holds, in token order; every row sums to 197 and its largest entry is 64.
All inputs are finite; a program needn't handle non-finite values.
Results may differ from a plain program's by a relative error of at most 0.011.
Values may be sent and summed in bfloat16 or wider, within the bound.
A program may use at most 128 MiB of HBM per device.

v0:
```python
import functools
import math

import jax
import jax.numpy as jnp
from jax import lax
from jax.experimental import pallas as pl
from jax.experimental.pallas import tpu as pltpu
from jax.sharding import PartitionSpec as P

LN_EPS = 1e-06
HALF_ROOT = 0.7071067811865476
INV_ROOT_TAU = 0.3989422804014327
F32 = jnp.float32
BF16 = jnp.bfloat16


def norm_statistics(values):
    centered = values - jnp.mean(values, axis=-1, keepdims=True)
    variance = jnp.mean(centered * centered, axis=-1, keepdims=True)
    inverse_deviation = lax.rsqrt(variance + LN_EPS)
    return (centered * inverse_deviation, inverse_deviation)


def norm_backward(incoming, gain, unit, inverse_deviation):
    scaled = incoming * gain
    return inverse_deviation * (
        scaled
        - jnp.mean(scaled, axis=-1, keepdims=True)
        - unit * jnp.mean(scaled * unit, axis=-1, keepdims=True)
    )


def gelu_parts(pre):
    cdf = 0.5 * (1.0 + lax.erf(pre * HALF_ROOT))
    density = jnp.exp(-0.5 * pre * pre) * INV_ROOT_TAU
    return (cdf, density)


def exchange_kernel(plan, *refs):
    count = len(plan)
    sources = refs[:count]
    outs = refs[count : 2 * count]
    landings = refs[2 * count : -2]
    send_sems, recv_sems = refs[-2:]
    sizes = {axis: size for axis, size, _ in plan}
    barrier = pltpu.get_barrier_semaphore()
    for axis, size in sizes.items():
        me = lax.axis_index(axis)
        for step in range(1, size):
            pl.semaphore_signal(
                barrier,
                inc=1,
                device_id={axis: lax.rem(me + step, size)},
                device_id_type=pl.DeviceIdType.MESH,
            )
    pl.semaphore_wait(barrier, sum(size - 1 for size in sizes.values()))
    copies = []
    landing = 0
    for i, (axis, size, reduced) in enumerate(plan):
        me = lax.axis_index(axis)
        for step in range(1, size):
            peer = lax.rem(me + step, size)
            if reduced:
                src, dst = sources[i].at[peer], landings[landing].at[step - 1]
            else:
                src, dst = sources[i], outs[i].at[me]
            copy = pltpu.make_async_remote_copy(
                src_ref=src,
                dst_ref=dst,
                send_sem=send_sems.at[len(copies)],
                recv_sem=recv_sems.at[len(copies)],
                device_id={axis: peer},
                device_id_type=pl.DeviceIdType.MESH,
            )
            copy.start()
            copies.append(copy)
        landing += int(reduced)
    for i, (axis, size, reduced) in enumerate(plan):
        me = lax.axis_index(axis)
        if reduced:
            outs[i][...] = sources[i][me].astype(F32)
        else:
            outs[i][me] = sources[i][...]
    landing, done = 0, 0
    for i, (axis, size, reduced) in enumerate(plan):
        for step in range(1, size):
            copies[done].wait()
            done += 1
            if reduced:
                outs[i][...] += landings[landing][step - 1].astype(F32)
        landing += int(reduced)


def exchange(collective_id, *items):
    plan = tuple((axis, size, reduced) for axis, size, reduced, _ in items)
    arrays = tuple(v for _, _, _, v in items)
    out_shape = [
        jax.ShapeDtypeStruct(v.shape[1:], F32)
        if reduced
        else jax.ShapeDtypeStruct((size,) + v.shape, v.dtype)
        for _, size, reduced, v in items
    ]
    copies = sum(size - 1 for _, size, _ in plan)
    return pl.pallas_call(
        functools.partial(exchange_kernel, plan),
        out_shape=out_shape,
        in_specs=[pl.BlockSpec(memory_space=pltpu.VMEM)] * len(arrays),
        out_specs=[pl.BlockSpec(memory_space=pltpu.VMEM)] * len(arrays),
        scratch_shapes=[
            pltpu.VMEM((size - 1,) + v.shape[1:], v.dtype)
            for _, size, reduced, v in items
            if reduced
        ]
        + [pltpu.SemaphoreType.DMA((copies,)), pltpu.SemaphoreType.DMA((copies,))],
        compiler_params=pltpu.CompilerParams(
            collective_id=collective_id, has_side_effects=True
        ),
    )(*arrays)


def softmax_of(q, k, mask, scale):
    scores = dot(q, k, 1, 1) * scale + mask
    top = jnp.max(scores, axis=1, keepdims=True)
    weights = jnp.exp(scores - top)
    return weights / jnp.sum(weights, axis=1, keepdims=True)


def attention_kernel(heads, head_dim, q_ref, k_ref, v_ref, mask_ref, o_ref):
    parts, _, cap, cols = q_ref.shape
    scale = 1.0 / math.sqrt(head_dim)
    mask = mask_ref[0]
    q, k, v = (r[...].reshape(parts * cap, cols) for r in (q_ref, k_ref, v_ref))
    pieces = []
    for h in range(heads):
        c = slice(h * head_dim, (h + 1) * head_dim)
        probs = softmax_of(q[:, c], k[:, c], mask, scale).astype(BF16)
        pieces.append(dot(probs, v[:, c], 1, 0).astype(BF16))
    o_ref[...] = jnp.concatenate(pieces, axis=1).reshape(o_ref.shape)


def attention_back_kernel(
    heads, head_dim, q_ref, k_ref, v_ref, do_ref, mask_ref, d_ref, sum_ref
):
    parts, _, cap, cols = q_ref.shape
    scale = 1.0 / math.sqrt(head_dim)
    mask = mask_ref[0]
    q, k, v, d = (r[...].reshape(parts * cap, cols) for r in (q_ref, k_ref, v_ref, do_ref))
    dq, dk, dv = [], [], []
    for h in range(heads):
        c = slice(h * head_dim, (h + 1) * head_dim)
        probs = softmax_of(q[:, c], k[:, c], mask, scale)
        dv.append(dot(probs.astype(BF16), d[:, c], 0, 0))
        d_probs = dot(d[:, c], v[:, c], 1, 1)
        delta = jnp.sum(probs * d_probs, axis=1, keepdims=True)
        d_scores = (probs * (d_probs - delta) * scale).astype(BF16)
        dq.append(dot(d_scores, k[:, c], 1, 0))
        dk.append(dot(d_scores, q[:, c], 0, 0))
    dq, dk, dv = (jnp.concatenate(p, axis=1) for p in (dq, dk, dv))
    d_ref[...] = jnp.concatenate([dq, dk, dv], axis=1).astype(BF16).reshape(d_ref.shape)
    sums = jnp.concatenate(
        [jnp.sum(dq, axis=0, keepdims=True), jnp.sum(dv, axis=0, keepdims=True)], axis=0
    )

    @pl.when(pl.program_id(0) == 0)
    def _():
        sum_ref[...] = sums

    @pl.when(pl.program_id(0) > 0)
    def _():
        sum_ref[...] += sums


def image_block(v, cols):
    return pl.BlockSpec((v[0], 1, v[1], cols), lambda i: (0, i, 0, 0))


def attention(q, k, v, mask, heads):
    parts, images, cap, cols = q.shape
    block = image_block((parts, cap), cols)
    return pl.pallas_call(
        functools.partial(attention_kernel, heads, cols // heads),
        grid=(images,),
        out_shape=jax.ShapeDtypeStruct(q.shape, BF16),
        in_specs=[block] * 3 + [pl.BlockSpec((1, 1, parts * cap), lambda i: (i, 0, 0))],
        out_specs=block,
    )(q, k, v, mask)


def attention_back(q, k, v, d, mask, heads):
    parts, images, cap, cols = q.shape
    block = image_block((parts, cap), cols)
    return pl.pallas_call(
        functools.partial(attention_back_kernel, heads, cols // heads),
        grid=(images,),
        out_shape=[
            jax.ShapeDtypeStruct((parts, images, cap, 3 * cols), BF16),
            jax.ShapeDtypeStruct((2, cols), F32),
        ],
        in_specs=[block] * 4 + [pl.BlockSpec((1, 1, parts * cap), lambda i: (i, 0, 0))],
        out_specs=[
            image_block((parts, cap), 3 * cols),
            pl.BlockSpec((2, cols), lambda i: (0, 0)),
        ],
    )(q, k, v, d, mask)


def gather_tensor(block):
    return lax.all_gather(block, "tensor", axis=0, tiled=False)


def scatter_dp(parts):
    return lax.psum_scatter(parts, "dp", scatter_dimension=0, tiled=True).astype(F32)


def dot(a, b, ca, cb):
    return lax.dot_general(a, b, (((ca,), (cb,)), ((), ())), preferred_element_type=F32)


def on_device(
    tokens, counts, w_qkv, b_qv, w_out, w_fc1, b_fc1, w_fc2, ln_gain, vec_bias, cotangent
):
    rank = lax.axis_index("tensor")
    images, cap, width = tokens.shape
    parts = counts.shape[1]
    heads, head_narrow = b_qv.shape[1], b_qv.shape[2]
    data = width // w_fc1.shape[0]
    head_dim = head_narrow * data
    cols = heads * head_dim
    hidden_cols = w_fc1.shape[1]
    narrow = width // data
    own_rows = images * cap
    rows = parts * own_rows
    scale = 1.0 / math.sqrt(head_dim)

    live = jnp.arange(cap, dtype=jnp.int32)[None, None, :] < counts.T[:, :, None]
    live_own = lax.dynamic_index_in_dim(live, rank, axis=0, keepdims=False)
    live_own = live_own.reshape(own_rows, 1)
    key_mask = jnp.where(live.transpose(1, 0, 2).reshape(images, 1, parts * cap), 0.0, -1e30)

    cot_own = jnp.where(live_own, cotangent.reshape(own_rows, width), jnp.zeros((), BF16))
    tok_own = tokens.reshape(own_rows, width)

    small = jnp.concatenate(
        [
            ln_gain.reshape(-1),
            vec_bias.reshape(-1),
            b_qv.reshape(-1),
            b_fc1.reshape(-1),
        ]
    )
    lanes = 3 * cols
    pad_rows = 16 * pl.cdiv(small.size, 16 * lanes)
    small_rows = jnp.pad(small, (0, pad_rows * lanes - small.size)).reshape(pad_rows, lanes)
    qkv_flat = w_qkv.transpose(1, 0, 2).reshape(narrow, lanes)
    tok_all, out_ranks, first = exchange(
        0,
        ("tensor", parts, False, tok_own),
        ("tensor", parts, False, w_out.T),
        ("dp", data, False, jnp.concatenate([qkv_flat, small_rows], axis=0)),
    )
    tok_all = tok_all.reshape(rows, width)
    qkv_all = first[:, :narrow].reshape(width, lanes)
    small_all = first[:, narrow:].reshape(data, pad_rows * lanes)[:, : small.size]
    mlp_all = lax.all_gather(
        jnp.concatenate([w_fc1, w_fc2.T], axis=1), "dp", axis=0, tiled=True
    )
    cot_all = gather_tensor(cot_own).reshape(rows, width)
    fc1 = mlp_all[:, :hidden_cols]
    fc2_t = mlp_all[:, hidden_cols:]

    n0 = 2 * narrow
    n1 = n0 + 4 * narrow
    n2 = n1 + 2 * cols // data
    gain = (
        small_all[:, :n0].reshape(data, 2, narrow).transpose(1, 0, 2).reshape(2, width).astype(F32)
    )
    bias = (
        small_all[:, n0:n1].reshape(data, 4, narrow).transpose(1, 0, 2).reshape(4, width).astype(F32)
    )
    bias_qv = (
        small_all[:, n1:n2]
        .reshape(data, 2 * heads, head_narrow)
        .transpose(1, 0, 2)
        .reshape(2, cols)
        .astype(F32)
    )
    bias_hidden = (
        small_all[:, n2:]
        .reshape(data, hidden_cols // head_dim, head_narrow)
        .transpose(1, 0, 2)
        .reshape(hidden_cols)
        .astype(F32)
    )

    unit1, inv1 = norm_statistics(tok_all.astype(F32))
    a1 = (unit1 * gain[0] + bias[0]).astype(BF16)
    projected = dot(a1, qkv_all, 1, 0)

    shape4 = (parts, images, cap, cols)
    queries = (projected[:, :cols] + bias_qv[0]).astype(BF16).reshape(shape4)
    keys = projected[:, cols : 2 * cols].astype(BF16).reshape(shape4)
    values = (projected[:, 2 * cols :] + bias_qv[1]).astype(BF16).reshape(shape4)
    attended = attention(queries, keys, values, key_mask, heads).reshape(rows, cols)
    attended_all, out_every = exchange(
        1,
        ("tensor", parts, False, attended),
        ("dp", data, False, out_ranks.transpose(1, 0, 2).reshape(narrow, parts * cols)),
    )
    out_every = out_every.reshape(width, parts * cols)
    out_all = lax.dynamic_slice_in_dim(out_every, rank * cols, cols, axis=1)
    attended_all = attended_all.transpose(1, 0, 2).reshape(rows, parts * cols)
    attn = dot(attended_all, out_every, 1, 1)
    resid = tok_all.astype(F32) + attn + bias[1]
    unit2, inv2 = norm_statistics(resid)
    a2 = (unit2 * gain[1] + bias[2]).astype(BF16)
    pre = dot(a2, fc1, 1, 0) + bias_hidden
    cdf, density = gelu_parts(pre)
    hidden = (pre * cdf).astype(BF16)
    d_hidden = dot(cot_all, fc2_t, 1, 0) * (cdf + pre * density)
    d_hidden_bf = d_hidden.astype(BF16)
    back2 = dot(d_hidden_bf, fc1, 1, 1)
    (d_a2,) = exchange(
        2, ("tensor", parts, True, back2.astype(BF16).reshape(parts, own_rows, width))
    )

    def own(full):
        return lax.dynamic_index_in_dim(
            full.reshape(parts, own_rows, full.shape[1]), rank, axis=0, keepdims=False
        )

    resid_own = own(resid)
    unit2_own, inv2_own = norm_statistics(resid_own)
    dy1 = jnp.where(
        live_own,
        cot_own.astype(F32) + norm_backward(d_a2, gain[1], unit2_own, inv2_own),
        0.0,
    )
    (dy1_all,) = exchange(3, ("tensor", parts, False, dy1.astype(BF16)))
    dy1_all = dy1_all.reshape(rows, width)

    mlp_out = dot(hidden, fc2_t, 1, 1).astype(BF16)
    mlp_own = lax.psum_scatter(
        mlp_out.reshape(parts, own_rows, width), "tensor", scatter_dimension=0, tiled=False
    ).astype(F32)
    result = jnp.where(live_own, resid_own + mlp_own + bias[3], 0.0).astype(BF16)
    g_fc1 = dot(a2, d_hidden_bf, 0, 0)
    g_fc2 = dot(cot_all, hidden, 0, 0)
    g_mlp = scatter_dp(jnp.concatenate([g_fc1.astype(BF16), g_fc2.astype(BF16)], axis=1))

    d_att = dot(dy1_all, out_all, 1, 0).astype(BF16).reshape(shape4)
    d_proj, g_bqv = attention_back(queries, keys, values, d_att, key_mask, heads)
    d_proj = d_proj.reshape(rows, lanes)
    back1 = dot(d_proj, qkv_all, 1, 1)
    g_qkv = dot(a1, d_proj, 0, 0)
    g_out = dot(dy1_all, attended, 0, 0)
    g_att = scatter_dp(jnp.concatenate([g_qkv.astype(BF16), g_out.astype(BF16)], axis=1))

    sums = jnp.stack(
        [
            jnp.sum(back1 * unit1, axis=0),
            jnp.sum(back2 * unit2, axis=0),
            jnp.sum(back1, axis=0),
            jnp.sum(dy1, axis=0),
            jnp.sum(back2, axis=0),
            jnp.sum(cot_own.astype(F32), axis=0),
        ]
    )
    sixth_parts = (
        sums.reshape(6, data, parts, narrow // parts)
        .transpose(2, 1, 0, 3)
        .reshape(parts, data, 6 * narrow // parts)
    )
    d_a1, sixth_sums = exchange(
        4,
        ("tensor", parts, True, back1.astype(BF16).reshape(parts, own_rows, width)),
        ("tensor", parts, True, sixth_parts),
    )
    lane = jnp.concatenate(
        [
            sixth_sums,
            g_bqv.reshape(2 * heads, data, head_narrow).transpose(1, 0, 2).reshape(data, -1),
            jnp.sum(d_hidden, axis=0)
            .reshape(hidden_cols // head_dim, data, head_narrow)
            .transpose(1, 0, 2)
            .reshape(data, -1),
        ],
        axis=1,
    )
    lane_size = lane.shape[1]
    lane_rows = 8 * pl.cdiv(lane_size, 1024)
    lane = jnp.pad(lane, ((0, 0), (0, lane_rows * 128 - lane_size)))
    (lane,) = exchange(5, ("dp", data, True, lane.reshape(data, lane_rows, 128)))
    lane = lane.reshape(-1)[:lane_size]
    m0 = 6 * narrow // parts
    m1 = m0 + 2 * cols // data
    sixth = lane[:m0].reshape(6, narrow // parts)

    unit1_own, inv1_own = norm_statistics(tok_own.astype(F32))
    grad_tokens = jnp.where(
        live_own, dy1 + norm_backward(d_a1, gain[0], unit1_own, inv1_own), 0.0
    ).astype(BF16)
    return (
        result.reshape(images, cap, width),
        grad_tokens.reshape(images, cap, width),
        g_att[:, : 3 * cols].reshape(narrow, 3, cols).transpose(1, 0, 2),
        g_att[:, 3 * cols :].T,
        g_mlp[:, :hidden_cols],
        g_mlp[:, hidden_cols:].T,
        lane[m0:m1].reshape(2, heads, head_narrow),
        lane[m1:lane_size].reshape(hidden_cols // head_dim, head_narrow),
        sixth[:2],
        sixth[2:],
    )


def solution(mesh):
    in_specs = (
        P("dp", "tensor", None),
        P("dp", None),
        P(None, "dp", "tensor"),
        P(None, "tensor", "dp"),
        P("tensor", "dp"),
        P("dp", "tensor"),
        P("tensor", "dp"),
        P("tensor", "dp"),
        P(None, "dp"),
        P(None, "dp"),
        P("dp", "tensor", None),
    )
    out_specs = (
        P("dp", "tensor", None),
        P("dp", "tensor", None),
        P(None, "dp", "tensor"),
        P("tensor", "dp"),
        P("dp", "tensor"),
        P("tensor", "dp"),
        P(None, "tensor", "dp"),
        P("tensor", "dp"),
        P(None, ("dp", "tensor")),
        P(None, ("dp", "tensor")),
    )
    return jax.shard_map(
        on_device, mesh=mesh, in_specs=in_specs, out_specs=out_specs, check_vma=False
    )
```

profile of v0, /device:TPU:0, one launch (start us, length us, event | category | flops | bytes accessed | tf_op | source)
XLA Modules:
  0.0 311.1 jit_solution(6953700980463319388)
XLA Ops:
  7.2 1.7 pad_maximum_fusion.2
  10.5 1.8 bitcast_select_fusion
  15.6 1.5 copy.61
  19.1 39.3 %shard_map.186 = (bf16[4,192,768]{2,1,0:T(8,128)(2,1)}, bf16[4,96,192]{2,1,0:T(8,128)(2,1)}, bf16[8,112,576]{2,1,0:T(8,128)(2,1)}) custom-call(bf16[192,768]{1,0:T(8,128)(2,1)} %bitcast.105, bf16[96,192]{1,0:T(8,128)(2,1)} %bitcast.132, bf16[112,576]{1,0:T(8,128)(2,1)} %pad_maximum_fusion.3.refs_2_), custom_call_target="tpu_custom_call" | custom-call | tf_op jit(solution)/shard_map/pallas_call | solution.py:105
  71.6 4.9 %shard_map.187 = bf16[4,3,64,192]{3,2,1,0:T(8,128)(2,1)} custom-call(bf16[4,3,64,192]{3,2,1,0:T(8,128)(2,1)} %bitcast.113, bf16[4,3,64,192]{3,2,1,0:T(8,128)(2,1)} %bitcast.111, bf16[4,3,64,192]{3,2,1,0:T(8,128)(2,1)} %bitcast.109, f32[3,1,256]{2,1,0:T(1,128)} %compare_select_fusion.mask_ref), custom_call_target="tpu_custom_call" | custom-call | tf_op jit(solution)/shard_map/pallas_call | solution.py:181
  76.4 32.6 %shard_map.188 = (bf16[4,768,192]{2,1,0:T(8,128)(2,1)}, bf16[8,96,768]{2,1,0:T(8,128)(2,1)}) custom-call(bf16[768,192]{1,0:T(8,128)(2,1)} %bitcast.107, bf16[96,768]{1,0:T(8,128)(2,1)} %reshape.462.refs_1_), custom_call_target="tpu_custom_call" | custom-call | tf_op jit(solution)/shard_map/pallas_call | solution.py:105
  109.0 2.5 copy.72
  111.5 2.9 fusion.44
  116.0 4.2 %multiply_convert_fusion = (bf16[768,768]{1,0:T(8,128)(2,1)S(1)}, f32[768,768]{1,0:T(8,128)}) fusion(f32[768]{0:T(1024)} %reshape.486, bf16[768,1536]{1,0:T(8,128)(2,1)} %all-gather.3.cloned.1.call-done, f32[768,768]{1,0:T(8,128)S(1)} %get-tuple-element.89, f32[768]{0:T(1024)} %add.166, f32[768]{0:T(1024)S(1)} %mul.178, f32[768]{0:T(1024)} %add_rsqrt_fusion, ...), kind=kOutput, calls=%fused_computation.22 | convolution fusion | flops 912457728 | bytes 7097344 | tf_op jit(solution)/shard_map/dot_general | solution.py:217
  120.2 2.1 convolution_convert_fusion.2
  128.3 2.9 convolution_convert_fusion
  131.7 2.8 fusion.45
  136.9 1.6 pad_maximum_fusion
  138.5 4.3 %copy.85 = bf16[768,1536]{1,0:T(8,128)(2,1)} copy(bf16[768,1536]{0,1:T(8,128)(2,1)} %pad_maximum_fusion) | data formatting | bytes 4718592
  142.8 4.5 %fusion.39 = (f32[768]{0:T(1024)}, f32[768]{0:T(1024)}, bf16[768,768]{1,0:T(8,128)(2,1)}) fusion(f32[768]{0:T(1024)} %add_rsqrt_fusion, f32[768,768]{1,0:T(8,128)S(1)} %get-tuple-element.89, f32[768]{0:T(1024)S(1)} %copy-done.13, bf16[768,1536]{1,0:T(8,128)(2,1)} %all-gather.3.cloned.1.call-done, bf16[768,768]{1,0:T(8,128)(2,1)} %copy-done.29), kind=kOutput, calls=%fused_computation.118 | convolution fusion | flops 909507072 | bytes 5911552 | tf_op jit(solution)/shard_map/dot_general | solution.py:217
  150.0 1.4 reshape.480
  151.4 1.4 copy.78
  152.9 1.5 reshape.481
  154.4 31.6 %shard_map.189 = f32[192,768]{1,0:T(8,128)} custom-call(bf16[4,192,768]{2,1,0:T(8,128)(2,1)} %bitcast.123), custom_call_target="tpu_custom_call" | custom-call | tf_op jit(solution)/shard_map/pallas_call | solution.py:105
  186.0 1.7 dynamic-slice_reduce_fusion
  187.7 1.8 convert_reduce_fusion.2
  192.5 2.3 fusion.41
  194.9 1.8 convert_element_type.174.refs_0_
  196.7 30.5 %shard_map.190 = bf16[4,192,768]{2,1,0:T(8,128)(2,1)} custom-call(bf16[192,768]{1,0:T(8,128)(2,1)} %convert_element_type.174.refs_0_), custom_call_target="tpu_custom_call" | custom-call | tf_op jit(solution)/shard_map/pallas_call | solution.py:105
  227.2 2.2 convolution_convert_fusion.5
  230.4 8.1 %shard_map.191 = (bf16[4,3,64,576]{3,2,1,0:T(8,128)(2,1)}, f32[2,192]{1,0:T(2,128)}) custom-call(bf16[4,3,64,192]{3,2,1,0:T(8,128)(2,1)} %bitcast.114, bf16[4,3,64,192]{3,2,1,0:T(8,128)(2,1)} %bitcast.112, bf16[4,3,64,192]{3,2,1,0:T(8,128)(2,1)} %bitcast.110, bf16[4,3,64,192]{3,2,1,0:T(8,128)(2,1)} %bitcast.118, f32[3,1,256]{2,1,0:T(1,128)} %compare_select_fusion.mask_ref), custom_call_target="tpu_custom_call" | custom-call | tf_op jit(solution)/shard_map/pallas_call | solution.py:193
  238.9 2.5 convolution_convert_fusion.3
  241.5 1.5 copy.83
  243.0 3.4 %fusion.40 = (f32[768]{0:T(1024)S(1)}, f32[768]{0:T(1024)S(1)}, bf16[768,768]{1,0:T(8,128)(2,1)}) fusion(f32[768]{0:T(1024)S(1)} %copy-done.21, f32[768]{0:T(1024)S(1)} %copy-done.20, bf16[4,192,768]{2,1,0:T(8,128)(2,1)S(1)} %copy-done.1, bf16[768,576]{1,0:T(8,128)(2,1)} %bitcast.151, bf16[768,576]{1,0:T(8,128)(2,1)S(1)} %bitcast.127), kind=kOutput, calls=%fused_computation.119 | convolution fusion | flops 683604480 | bytes 4141056 | tf_op jit(solution)/shard_map/dot_general | solution.py:217
  247.7 35.2 %shard_map.192 = (f32[192,768]{1,0:T(8,128)}, f32[8,144]{1,0:T(8,128)}) custom-call(bf16[4,192,768]{2,1,0:T(8,128)(2,1)} %bitcast.122, f32[4,8,144]{2,1,0:T(8,128)} %reshape.475.refs_1_), custom_call_target="tpu_custom_call" | custom-call | tf_op jit(solution)/shard_map/pallas_call | solution.py:105
  284.4 6.0 %shard_map.193 = f32[8,128]{1,0:T(8,128)} custom-call(f32[8,8,128]{2,1,0:T(8,128)} %bitcast.140), custom_call_target="tpu_custom_call" | custom-call | tf_op jit(solution)/shard_map/pallas_call | solution.py:105
  296.7 2.0 select_convert_fusion
  (200 shorter events, 52.3 us)
Async XLA Ops:
  7.2 108.8 %all-gather.3.cloned.1.call-start = ((), (), s32[]{:S(2)}) async-start(), calls=%async_computation.3 | async-start | bytes 2654208 | tf_op jit(solution)/shard_map/all_gather | solution.py:265
  9.0 119.3 %all-gather.5.cloned.1.call-start = ((), (), s32[]{:S(2)}) async-start(), calls=%async_computation.5 | async-start | bytes 1474560 | tf_op jit(solution)/shard_map/all_gather | solution.py:209
  10.5 2.6 copy-start.18
  12.2 49.0 %copy-start.17 = (s32[3,4]{1,0:T(4,128)S(1)}, s32[3,4]{1,0:T(4,128)}, u32[]{:S(2)}) copy-start(s32[3,4]{1,0:T(4,128)} %param.12) | copy-start | bytes 148
  12.3 173.8 %reduce-scatter.8.cloned.1.call-start = ((), (), s32[]{:S(2)}) async-start(), calls=%async_computation.4 | async-start | bytes 1474560 | tf_op jit(solution)/shard_map/reduce_scatter | solution.py:343
  58.4 3.0 copy-start.8
  58.4 4.0 %copy-start.1 = (bf16[4,192,768]{2,1,0:T(8,128)(2,1)S(1)}, bf16[4,192,768]{2,1,0:T(8,128)(2,1)}, u32[]{:S(2)}) copy-start(bf16[4,192,768]{2,1,0:T(8,128)(2,1)} %get-tuple-element.19) | copy-start | bytes 3538948
  60.7 6.4 %copy-start.6 = (bf16[8,96,576]{2,1,0:T(8,128)(2,1)}, bf16[8,96,576]{2,1,0:T(8,128)(2,1)S(1)}, u32[]{:S(2)}) copy-start(bf16[8,96,576]{2,1,0:T(8,128)(2,1)S(1)} %slice.122) | copy-start | bytes 2654212
  116.0 4.2 %copy-start.26 = (bf16[768,1536]{1,0:T(8,128)(2,1)S(1)}, bf16[768,1536]{1,0:T(8,128)(2,1)}, u32[]{:S(2)}) copy-start(bf16[768,1536]{1,0:T(8,128)(2,1)} %all-gather.3.cloned.1.call-done) | copy-start | bytes 7077892
  120.2 2.1 copy-start.30
  122.3 176.5 %reduce-scatter.12.cloned.1.call-start = ((), (), s32[]{:S(2)}) async-start(), calls=%async_computation.7 | async-start | bytes 2654208
  128.2 2.9 copy-start.24
  128.2 3.0 copy-start.27
  128.3 3.0 copy-start.28
  128.3 3.4 %copy-start.31 = (f32[768,768]{1,0:T(8,128)S(1)}, f32[768,768]{1,0:T(8,128)}, u32[]{:S(2)}) copy-start(f32[768,768]{1,0:T(8,128)} %get-tuple-element.92) | copy-start | bytes 7077892
  131.7 3.8 %copy-start.13 = (f32[768]{0:T(1024)S(1)}, f32[768]{0:T(1024)}, u32[]{:S(2)}) copy-start(f32[768]{0:T(1024)} %copy-done.12) | copy-start | bytes 9220
  131.7 3.8 %copy-start.22 = (f32[768]{0:T(1024)S(1)}, f32[768]{0:T(1024)}, u32[]{:S(2)}) copy-start(f32[768]{0:T(1024)} %add.166) | copy-start | bytes 9220
  131.7 3.8 %copy-start.23 = (f32[768]{0:T(1024)S(1)}, f32[768]{0:T(1024)}, u32[]{:S(2)}) copy-start(f32[768]{0:T(1024)} %add_rsqrt_fusion) | copy-start | bytes 9220
  142.8 159.1 %reduce-scatter.10.cloned.1.call-start = ((), (), s32[]{:S(2)}) async-start(), calls=%async_computation.6 | async-start | bytes 1327104
  227.2 11.3 %copy-start = (bf16[4,192,768]{2,1,0:T(8,128)(2,1)S(1)}, bf16[4,192,768]{2,1,0:T(8,128)(2,1)}, u32[]{:S(2)}) copy-start(bf16[4,192,768]{2,1,0:T(8,128)(2,1)} %shard_map.190) | copy-start | bytes 3538948
  227.2 11.3 %copy-start.4 = (bf16[4,3,64,192]{3,2,1,0:T(8,128)(2,1)S(1)}, bf16[4,3,64,192]{3,2,1,0:T(8,128)(2,1)}, u32[]{:S(2)}) copy-start(bf16[4,3,64,192]{3,2,1,0:T(8,128)(2,1)} %shard_map.187) | copy-start | bytes 884740
  241.4 1.6 copy-start.7
  242.9 3.7 %copy-start.25 = (f32[2,192]{1,0:T(2,128)S(1)}, f32[2,192]{1,0:T(2,128)}, u32[]{:S(2)}) copy-start(f32[2,192]{1,0:T(2,128)} %get-tuple-element.27) | copy-start | bytes 4612
  243.0 3.9 %copy-start.10 = (f32[1,8,4,24]{3,2,1,0:T(4,128)S(1)}, f32[1,8,4,24]{3,2,1,0:T(4,128)}, u32[]{:S(2)}) copy-start(f32[1,8,4,24]{3,2,1,0:T(4,128)} %stack.22) | copy-start | bytes 9220
  243.0 4.0 %copy-start.9 = (f32[1,8,4,24]{3,2,1,0:T(4,128)S(1)}, f32[1,8,4,24]{3,2,1,0:T(4,128)}, u32[]{:S(2)}) copy-start(f32[1,8,4,24]{3,2,1,0:T(4,128)} %stack.25) | copy-start | bytes 9220
  243.0 4.0 %copy-start.11 = (f32[1,8,4,24]{3,2,1,0:T(4,128)S(1)}, f32[1,8,4,24]{3,2,1,0:T(4,128)}, u32[]{:S(2)}) copy-start(f32[1,8,4,24]{3,2,1,0:T(4,128)} %stack.26) | copy-start | bytes 9220
  246.4 36.5 %copy-start.14 = (f32[8,96]{1,0:T(8,128)S(1)}, f32[8,96]{1,0:T(8,128)}, u32[]{:S(2)}) copy-start(f32[8,96]{1,0:T(8,128)} %reshape.481) | copy-start | bytes 9220
  246.4 48.9 %copy-start.2 = (bf16[3,64,768]{2,1,0:T(8,128)(2,1)S(1)}, bf16[3,64,768]{2,1,0:T(8,128)(2,1)}, u32[]{:S(2)}) copy-start(bf16[3,64,768]{2,1,0:T(8,128)(2,1)} %param.11) | copy-start | bytes 884740
  246.4 48.9 %copy-start.15 = (f32[192]{0:T(256)S(1)}, f32[192]{0:T(256)}, u32[]{:S(2)}) copy-start(f32[192]{0:T(256)} %div.52) | copy-start | bytes 2308
  246.4 48.9 %copy-start.16 = (f32[192]{0:T(256)S(1)}, f32[192]{0:T(256)}, u32[]{:S(2)}) copy-start(f32[192]{0:T(256)} %rsqrt.43) | copy-start | bytes 2308
  246.4 50.3 %copy-start.3 = (f32[192,768]{1,0:T(8,128)S(1)}, f32[192,768]{1,0:T(8,128)}, u32[]{:S(2)}) copy-start(f32[192,768]{1,0:T(8,128)} %get-tuple-element.73) | copy-start | bytes 1769476
  246.5 50.3 %copy-start.19 = (pred[192]{0:T(512)(128)(4,1)S(1)}, pred[192]{0:T(512)(128)(4,1)}, u32[]{:S(2)}) copy-start(pred[192]{0:T(512)(128)(4,1)} %copy-done.18) | copy-start | bytes 580
  (5 other events, 5.8 us)
Sparse Core Ops, SparseCore 0:
  10.4 37.6 all-gather.2
  50.2 30.2 all-gather.4
  122.4 35.8 reduce-scatter.7
  161.5 40.9 reduce-scatter.11
  247.0 40.4 reduce-scatter.9
where the time goes:
time: 313 us; the launch traced here: 311 us
  Pallas kernels  188 us (60%)
  local copies, waits for them, and re-layouts  51.9 us (17%)
  matrix products  30.1 us (10%)
  other arithmetic  26 us (8%)
  between operations  14.5 us (5%)
    pallas_call x6, Pallas kernels, exchange(): pl.pallas_call(functools.partial(exchange_kernel, plan), out_shape=out_sh...  175 us
    dot_general x12, matrix products, dot(): lax.dot_general(a, b, (((ca,), (cb,)), ((), ())), preferred_element_type=...  30.1 us
    unnamed x81, local copies, waits for them, and re-layouts  16.9 us
    pallas_call x1, Pallas kernels, attention_back(): pl.pallas_call(functools.partial(attention_back_kernel, heads, cols // he...  8.09 us
  transfers between devices with their start and end apart: 5, of which 0 were waited for; matrix products, arithmetic and copies ran while one was open for 33% of the time, Pallas kernels for 60%

commit v1 on v0

--- a/solution.py
+++ b/solution.py
@@ -55,9 +55,13 @@
                 device_id_type=pl.DeviceIdType.MESH,
             )
     pl.semaphore_wait(barrier, sum(size - 1 for size in sizes.values()))
-    copies = []
-    landing = 0
+    direct, used, landing = [], 0, 0
+    chains = []
     for i, (axis, size, reduced) in enumerate(plan):
+        if axis == "tensor" and not reduced:
+            chains.append((i, used))
+            used += 2 * (size - 1)
+            continue
         me = lax.axis_index(axis)
         for step in range(1, size):
             peer = lax.rem(me + step, size)
@@ -68,28 +72,73 @@
             copy = pltpu.make_async_remote_copy(
                 src_ref=src,
                 dst_ref=dst,
-                send_sem=send_sems.at[len(copies)],
-                recv_sem=recv_sems.at[len(copies)],
+                send_sem=send_sems.at[used],
+                recv_sem=recv_sems.at[used],
                 device_id={axis: peer},
                 device_id_type=pl.DeviceIdType.MESH,
             )
             copy.start()
-            copies.append(copy)
+            direct.append((i, step, landing, copy))
+            used += 1
         landing += int(reduced)
+
+    def hop(i, first_sem, step, way):
+        size = plan[i][1]
+        me = lax.axis_index("tensor")
+        block = lax.rem(me - way * step + size, size)
+        slot = first_sem + 2 * step + (way + 1) // 2
+        return pltpu.make_async_remote_copy(
+            src_ref=sources[i] if step == 0 else outs[i].at[block],
+            dst_ref=outs[i].at[block],
+            send_sem=send_sems.at[slot],
+            recv_sem=recv_sems.at[slot],
+            device_id={"tensor": lax.rem(me + way + size, size)},
+            device_id_type=pl.DeviceIdType.MESH,
+        )
+
+    def each_hop(step, act):
+        for i, first_sem in chains:
+            size = plan[i][1]
+            me = lax.axis_index("tensor")
+            act(i, first_sem, 1, me, size - 1 - me)
+            act(i, first_sem, -1, size - 1 - me, me)
+
+    for step in range(max([plan[i][1] - 1 for i, _ in chains], default=0)):
+
+        def begin(i, first_sem, way, behind, ahead):
+            @pl.when((behind >= step) & (ahead >= 1))
+            def _():
+                hop(i, first_sem, step, way).start()
+
+        def arrive(i, first_sem, way, behind, ahead):
+            @pl.when(behind >= step + 1)
+            def _():
+                hop(i, first_sem, step, way).wait_recv()
+
+        each_hop(step, begin)
+        if step == 0:
+            for i, (axis, size, reduced) in enumerate(plan):
+                if not reduced:
+                    outs[i][lax.axis_index(axis)] = sources[i][...]
+        each_hop(step, arrive)
     for i, (axis, size, reduced) in enumerate(plan):
         me = lax.axis_index(axis)
         if reduced:
             outs[i][...] = sources[i][me].astype(F32)
-        else:
+        elif not chains:
             outs[i][me] = sources[i][...]
-    landing, done = 0, 0
-    for i, (axis, size, reduced) in enumerate(plan):
-        for step in range(1, size):
-            copies[done].wait()
-            done += 1
-            if reduced:
-                outs[i][...] += landings[landing][step - 1].astype(F32)
-        landing += int(reduced)
+    for i, step, landing, copy in direct:
+        copy.wait()
+        if plan[i][2]:
+            outs[i][...] += landings[landing][step - 1].astype(F32)
+    for step in range(max([plan[i][1] - 1 for i, _ in chains], default=0)):
+
+        def end(i, first_sem, way, behind, ahead):
+            @pl.when((behind >= step) & (ahead >= 1))
+            def _():
+                hop(i, first_sem, step, way).wait_send()
+
+        each_hop(step, end)
 
 
 def exchange(collective_id, *items):
@@ -101,7 +150,7 @@
         else jax.ShapeDtypeStruct((size,) + v.shape, v.dtype)
         for _, size, reduced, v in items
     ]
-    copies = sum(size - 1 for _, size, _ in plan)
+    copies = 2 * sum(size - 1 for _, size, _ in plan)
     return pl.pallas_call(
         functools.partial(exchange_kernel, plan),
         out_shape=out_shape,

time: 313 us -> 300 us (0.958)
  Pallas kernels: 188 us -> 175 us
    pallas_call x6, Pallas kernels: 175 us -> 162 us  [exchange(): pl.pallas_call(functools.partial(exchange_kernel, plan), out_shape=out_sh...]
  transfers between devices with their start and end apart: 5 -> 5, of which waited for: 0 -> 0; matrix products, arithmetic and copies ran while one was open for 33% -> 34% of each run, Pallas kernels for 60% -> 59%
where the time goes in v1:
time: 300 us; the launch traced here: 298 us
  Pallas kernels  175 us (58%)
  local copies, waits for them, and re-layouts  52 us (17%)
  matrix products  30.1 us (10%)
  other arithmetic  26 us (9%)
  between operations  14.5 us (5%)
    pallas_call x6, Pallas kernels, exchange(): pl.pallas_call(functools.partial(exchange_kernel, plan), out_shape=out_sh...  162 us
    dot_general x12, matrix products, dot(): lax.dot_general(a, b, (((ca,), (cb,)), ((), ())), preferred_element_type=...  30.1 us
    unnamed x81, local copies, waits for them, and re-layouts  16.9 us
    pallas_call x1, Pallas kernels, attention_back(): pl.pallas_call(functools.partial(attention_back_kernel, heads, cols // he...  8.08 us
  transfers between devices with their start and end apart: 5, of which 0 were waited for; matrix products, arithmetic and copies ran while one was open for 34% of the time, Pallas kernels for 59%

profile of v1, /device:TPU:0, one launch (start us, length us, event | category | flops | bytes accessed | tf_op | source)
XLA Modules:
  0.0 297.9 jit_solution(10335280352284213532)
XLA Ops:
  7.2 1.7 pad_maximum_fusion.2
  10.5 1.8 bitcast_select_fusion
  15.6 1.5 copy.61
  19.1 35.2 %shard_map.186 = (bf16[4,192,768]{2,1,0:T(8,128)(2,1)}, bf16[4,96,192]{2,1,0:T(8,128)(2,1)}, bf16[8,112,576]{2,1,0:T(8,128)(2,1)}) custom-call(bf16[192,768]{1,0:T(8,128)(2,1)} %bitcast.105, bf16[96,192]{1,0:T(8,128)(2,1)} %bitcast.132, bf16[112,576]{1,0:T(8,128)(2,1)} %pad_maximum_fusion.3.refs_2_), custom_call_target="tpu_custom_call" | custom-call | tf_op jit(solution)/shard_map/pallas_call | solution.py:154
  67.5 4.9 %shard_map.187 = bf16[4,3,64,192]{3,2,1,0:T(8,128)(2,1)} custom-call(bf16[4,3,64,192]{3,2,1,0:T(8,128)(2,1)} %bitcast.113, bf16[4,3,64,192]{3,2,1,0:T(8,128)(2,1)} %bitcast.111, bf16[4,3,64,192]{3,2,1,0:T(8,128)(2,1)} %bitcast.109, f32[3,1,256]{2,1,0:T(1,128)} %compare_select_fusion.mask_ref), custom_call_target="tpu_custom_call" | custom-call | tf_op jit(solution)/shard_map/pallas_call | solution.py:230
  72.3 37.1 %shard_map.188 = (bf16[4,768,192]{2,1,0:T(8,128)(2,1)}, bf16[8,96,768]{2,1,0:T(8,128)(2,1)}) custom-call(bf16[768,192]{1,0:T(8,128)(2,1)} %bitcast.107, bf16[96,768]{1,0:T(8,128)(2,1)} %reshape.462.refs_1_), custom_call_target="tpu_custom_call" | custom-call | tf_op jit(solution)/shard_map/pallas_call | solution.py:154
  109.5 2.5 copy.72
  112.0 2.9 fusion.44
  116.5 4.2 %multiply_convert_fusion = (bf16[768,768]{1,0:T(8,128)(2,1)S(1)}, f32[768,768]{1,0:T(8,128)}) fusion(f32[768]{0:T(1024)} %reshape.486, bf16[768,1536]{1,0:T(8,128)(2,1)} %all-gather.3.cloned.1.call-done, f32[768,768]{1,0:T(8,128)S(1)} %get-tuple-element.89, f32[768]{0:T(1024)} %add.166, f32[768]{0:T(1024)S(1)} %mul.178, f32[768]{0:T(1024)} %add_rsqrt_fusion, ...), kind=kOutput, calls=%fused_computation.22 | convolution fusion | flops 912457728 | bytes 7097344 | tf_op jit(solution)/shard_map/dot_general | solution.py:266
  120.6 2.1 convolution_convert_fusion.2
  128.8 2.9 convolution_convert_fusion
  132.3 2.7 fusion.45
  137.4 1.6 pad_maximum_fusion
  139.0 4.3 %copy.85 = bf16[768,1536]{1,0:T(8,128)(2,1)} copy(bf16[768,1536]{0,1:T(8,128)(2,1)} %pad_maximum_fusion) | data formatting | bytes 4718592
  143.4 4.5 %fusion.39 = (f32[768]{0:T(1024)}, f32[768]{0:T(1024)}, bf16[768,768]{1,0:T(8,128)(2,1)}) fusion(f32[768]{0:T(1024)} %add_rsqrt_fusion, f32[768,768]{1,0:T(8,128)S(1)} %get-tuple-element.89, f32[768]{0:T(1024)S(1)} %copy-done.13, bf16[768,1536]{1,0:T(8,128)(2,1)} %all-gather.3.cloned.1.call-done, bf16[768,768]{1,0:T(8,128)(2,1)} %copy-done.29), kind=kOutput, calls=%fused_computation.118 | convolution fusion | flops 909507072 | bytes 5911552 | tf_op jit(solution)/shard_map/dot_general | solution.py:266
  150.6 1.4 reshape.480
  152.0 1.4 copy.78
  153.4 1.5 reshape.481
  155.0 24.1 %shard_map.189 = f32[192,768]{1,0:T(8,128)} custom-call(bf16[4,192,768]{2,1,0:T(8,128)(2,1)} %bitcast.123), custom_call_target="tpu_custom_call" | custom-call | tf_op jit(solution)/shard_map/pallas_call | solution.py:154
  179.1 1.7 dynamic-slice_reduce_fusion
  180.8 1.8 convert_reduce_fusion.2
  185.6 2.3 fusion.41
  187.9 1.8 convert_element_type.174.refs_0_
  189.8 27.7 %shard_map.190 = bf16[4,192,768]{2,1,0:T(8,128)(2,1)} custom-call(bf16[192,768]{1,0:T(8,128)(2,1)} %convert_element_type.174.refs_0_), custom_call_target="tpu_custom_call" | custom-call | tf_op jit(solution)/shard_map/pallas_call | solution.py:154
  217.5 2.2 convolution_convert_fusion.5
  220.6 8.1 %shard_map.191 = (bf16[4,3,64,576]{3,2,1,0:T(8,128)(2,1)}, f32[2,192]{1,0:T(2,128)}) custom-call(bf16[4,3,64,192]{3,2,1,0:T(8,128)(2,1)} %bitcast.114, bf16[4,3,64,192]{3,2,1,0:T(8,128)(2,1)} %bitcast.112, bf16[4,3,64,192]{3,2,1,0:T(8,128)(2,1)} %bitcast.110, bf16[4,3,64,192]{3,2,1,0:T(8,128)(2,1)} %bitcast.118, f32[3,1,256]{2,1,0:T(1,128)} %compare_select_fusion.mask_ref), custom_call_target="tpu_custom_call" | custom-call | tf_op jit(solution)/shard_map/pallas_call | solution.py:242
  229.2 2.5 convolution_convert_fusion.3
  231.7 1.5 copy.83
  233.3 3.4 %fusion.40 = (f32[768]{0:T(1024)S(1)}, f32[768]{0:T(1024)S(1)}, bf16[768,768]{1,0:T(8,128)(2,1)}) fusion(f32[768]{0:T(1024)S(1)} %copy-done.21, f32[768]{0:T(1024)S(1)} %copy-done.20, bf16[4,192,768]{2,1,0:T(8,128)(2,1)S(1)} %copy-done.1, bf16[768,576]{1,0:T(8,128)(2,1)} %bitcast.151, bf16[768,576]{1,0:T(8,128)(2,1)S(1)} %bitcast.127), kind=kOutput, calls=%fused_computation.119 | convolution fusion | flops 683604480 | bytes 4141056 | tf_op jit(solution)/shard_map/dot_general | solution.py:266
  238.0 29.7 %shard_map.192 = (f32[192,768]{1,0:T(8,128)}, f32[8,144]{1,0:T(8,128)}) custom-call(bf16[4,192,768]{2,1,0:T(8,128)(2,1)} %bitcast.122, f32[4,8,144]{2,1,0:T(8,128)} %reshape.475.refs_1_), custom_call_target="tpu_custom_call" | custom-call | tf_op jit(solution)/shard_map/pallas_call | solution.py:154
  269.1 8.1 %shard_map.193 = f32[8,128]{1,0:T(8,128)} custom-call(f32[8,8,128]{2,1,0:T(8,128)} %bitcast.140), custom_call_target="tpu_custom_call" | custom-call | tf_op jit(solution)/shard_map/pallas_call | solution.py:154
  283.6 2.0 select_convert_fusion
  (200 shorter events, 52.3 us)
Async XLA Ops:
  7.2 109.3 %all-gather.3.cloned.1.call-start = ((), (), s32[]{:S(2)}) async-start(), calls=%async_computation.3 | async-start | bytes 2654208 | tf_op jit(solution)/shard_map/all_gather | solution.py:314
  9.0 119.8 %all-gather.5.cloned.1.call-start = ((), (), s32[]{:S(2)}) async-start(), calls=%async_computation.5 | async-start | bytes 1474560 | tf_op jit(solution)/shard_map/all_gather | solution.py:258
  10.5 2.6 copy-start.18
  12.2 44.9 %copy-start.17 = (s32[3,4]{1,0:T(4,128)S(1)}, s32[3,4]{1,0:T(4,128)}, u32[]{:S(2)}) copy-start(s32[3,4]{1,0:T(4,128)} %param.12) | copy-start | bytes 148
  12.3 166.9 %reduce-scatter.8.cloned.1.call-start = ((), (), s32[]{:S(2)}) async-start(), calls=%async_computation.4 | async-start | bytes 1474560 | tf_op jit(solution)/shard_map/reduce_scatter | solution.py:392
  54.2 3.0 %copy-start.8 = (bf16[4,96,192]{2,1,0:T(8,128)(2,1)S(1)}, bf16[4,96,192]{2,1,0:T(8,128)(2,1)}, u32[]{:S(2)}) copy-start(bf16[4,96,192]{2,1,0:T(8,128)(2,1)} %get-tuple-element.21) | copy-start | bytes 442372
  54.3 4.0 %copy-start.1 = (bf16[4,192,768]{2,1,0:T(8,128)(2,1)S(1)}, bf16[4,192,768]{2,1,0:T(8,128)(2,1)}, u32[]{:S(2)}) copy-start(bf16[4,192,768]{2,1,0:T(8,128)(2,1)} %get-tuple-element.19) | copy-start | bytes 3538948
  56.6 6.4 %copy-start.6 = (bf16[8,96,576]{2,1,0:T(8,128)(2,1)}, bf16[8,96,576]{2,1,0:T(8,128)(2,1)S(1)}, u32[]{:S(2)}) copy-start(bf16[8,96,576]{2,1,0:T(8,128)(2,1)S(1)} %slice.122) | copy-start | bytes 2654212
  116.5 4.2 %copy-start.26 = (bf16[768,1536]{1,0:T(8,128)(2,1)S(1)}, bf16[768,1536]{1,0:T(8,128)(2,1)}, u32[]{:S(2)}) copy-start(bf16[768,1536]{1,0:T(8,128)(2,1)} %all-gather.3.cloned.1.call-done) | copy-start | bytes 7077892
  120.6 2.1 copy-start.30
  122.8 162.9 %reduce-scatter.12.cloned.1.call-start = ((), (), s32[]{:S(2)}) async-start(), calls=%async_computation.7 | async-start | bytes 2654208
  128.7 3.0 copy-start.24
  128.7 3.0 %copy-start.27 = (bf16[768,1536]{1,0:T(8,128)(2,1)S(1)}, bf16[768,1536]{1,0:T(8,128)(2,1)}, u32[]{:S(2)}) copy-start(bf16[768,1536]{1,0:T(8,128)(2,1)} %all-gather.3.cloned.1.call-done) | copy-start | bytes 7077892
  128.7 3.0 %copy-start.28 = (bf16[4,192,768]{2,1,0:T(8,128)(2,1)S(1)}, bf16[4,192,768]{2,1,0:T(8,128)(2,1)}, u32[]{:S(2)}) copy-start(bf16[4,192,768]{2,1,0:T(8,128)(2,1)} %all-gather.5.cloned.1.call-done) | copy-start | bytes 3538948
  128.7 3.5 %copy-start.31 = (f32[768,768]{1,0:T(8,128)S(1)}, f32[768,768]{1,0:T(8,128)}, u32[]{:S(2)}) copy-start(f32[768,768]{1,0:T(8,128)} %get-tuple-element.92) | copy-start | bytes 7077892
  132.3 3.8 %copy-start.13 = (f32[768]{0:T(1024)S(1)}, f32[768]{0:T(1024)}, u32[]{:S(2)}) copy-start(f32[768]{0:T(1024)} %copy-done.12) | copy-start | bytes 9220
  132.3 3.8 %copy-start.22 = (f32[768]{0:T(1024)S(1)}, f32[768]{0:T(1024)}, u32[]{:S(2)}) copy-start(f32[768]{0:T(1024)} %add.166) | copy-start | bytes 9220
  132.3 3.8 %copy-start.23 = (f32[768]{0:T(1024)S(1)}, f32[768]{0:T(1024)}, u32[]{:S(2)}) copy-start(f32[768]{0:T(1024)} %add_rsqrt_fusion) | copy-start | bytes 9220
  143.3 145.4 %reduce-scatter.10.cloned.1.call-start = ((), (), s32[]{:S(2)}) async-start(), calls=%async_computation.6 | async-start | bytes 1327104
  217.4 11.3 %copy-start = (bf16[4,192,768]{2,1,0:T(8,128)(2,1)S(1)}, bf16[4,192,768]{2,1,0:T(8,128)(2,1)}, u32[]{:S(2)}) copy-start(bf16[4,192,768]{2,1,0:T(8,128)(2,1)} %shard_map.190) | copy-start | bytes 3538948
  217.5 11.3 %copy-start.4 = (bf16[4,3,64,192]{3,2,1,0:T(8,128)(2,1)S(1)}, bf16[4,3,64,192]{3,2,1,0:T(8,128)(2,1)}, u32[]{:S(2)}) copy-start(bf16[4,3,64,192]{3,2,1,0:T(8,128)(2,1)} %shard_map.187) | copy-start | bytes 884740
  231.6 1.6 copy-start.7
  233.2 3.7 %copy-start.25 = (f32[2,192]{1,0:T(2,128)S(1)}, f32[2,192]{1,0:T(2,128)}, u32[]{:S(2)}) copy-start(f32[2,192]{1,0:T(2,128)} %get-tuple-element.27) | copy-start | bytes 4612
  233.2 3.9 %copy-start.10 = (f32[1,8,4,24]{3,2,1,0:T(4,128)S(1)}, f32[1,8,4,24]{3,2,1,0:T(4,128)}, u32[]{:S(2)}) copy-start(f32[1,8,4,24]{3,2,1,0:T(4,128)} %stack.22) | copy-start | bytes 9220
  233.2 4.0 %copy-start.9 = (f32[1,8,4,24]{3,2,1,0:T(4,128)S(1)}, f32[1,8,4,24]{3,2,1,0:T(4,128)}, u32[]{:S(2)}) copy-start(f32[1,8,4,24]{3,2,1,0:T(4,128)} %stack.25) | copy-start | bytes 9220
  233.2 4.0 %copy-start.11 = (f32[1,8,4,24]{3,2,1,0:T(4,128)S(1)}, f32[1,8,4,24]{3,2,1,0:T(4,128)}, u32[]{:S(2)}) copy-start(f32[1,8,4,24]{3,2,1,0:T(4,128)} %stack.26) | copy-start | bytes 9220
  236.7 31.0 %copy-start.14 = (f32[8,96]{1,0:T(8,128)S(1)}, f32[8,96]{1,0:T(8,128)}, u32[]{:S(2)}) copy-start(f32[8,96]{1,0:T(8,128)} %reshape.481) | copy-start | bytes 9220
  236.7 45.6 %copy-start.2 = (bf16[3,64,768]{2,1,0:T(8,128)(2,1)S(1)}, bf16[3,64,768]{2,1,0:T(8,128)(2,1)}, u32[]{:S(2)}) copy-start(bf16[3,64,768]{2,1,0:T(8,128)(2,1)} %param.11) | copy-start | bytes 884740
  236.7 45.6 %copy-start.15 = (f32[192]{0:T(256)S(1)}, f32[192]{0:T(256)}, u32[]{:S(2)}) copy-start(f32[192]{0:T(256)} %div.52) | copy-start | bytes 2308
  236.7 45.6 %copy-start.16 = (f32[192]{0:T(256)S(1)}, f32[192]{0:T(256)}, u32[]{:S(2)}) copy-start(f32[192]{0:T(256)} %rsqrt.43) | copy-start | bytes 2308
  236.7 46.9 %copy-start.3 = (f32[192,768]{1,0:T(8,128)S(1)}, f32[192,768]{1,0:T(8,128)}, u32[]{:S(2)}) copy-start(f32[192,768]{1,0:T(8,128)} %get-tuple-element.73) | copy-start | bytes 1769476
  236.7 46.9 %copy-start.19 = (pred[192]{0:T(512)(128)(4,1)S(1)}, pred[192]{0:T(512)(128)(4,1)}, u32[]{:S(2)}) copy-start(pred[192]{0:T(512)(128)(4,1)} %copy-done.18) | copy-start | bytes 580
  (5 other events, 5.8 us)
Sparse Core Ops, SparseCore 0:
  10.4 37.6 all-gather.2
  50.2 32.0 all-gather.4
  122.9 29.6 reduce-scatter.7
  155.8 40.9 reduce-scatter.11
  237.3 38.3 reduce-scatter.9
